TPU v7x, 32 devices: a whole 2x2x4 slice. The times are simulated.
32 devices in a mesh: seq: 4 (over z), head: 4 (over y, x), batch: 2 (over core).
Axes of the slice: x: 2, y: 2, z: 4, core: 2. Of those that a mesh axis runs over, the one named last changes fastest.
Arguments:
- hidden_in: float32 [2, 512, 768], P('batch', 'seq'), may hold values from -6 to 6
- cotangent: float32 [2, 512, 768], P('batch', 'seq'), may hold values from -6 to 6
- norm_gain: float32 [2, 768], replicated, may hold values from 0.5 to 1.5
- gate_proj: bfloat16 [2, 768, 1536], P(None, None, 'head'), may hold values from -0.21875 to 0.21875
- value_proj: bfloat16 [2, 768, 1536], P(None, None, 'head'), may hold values from -0.21875 to 0.21875
- shared_proj: bfloat16 [2, 768, 256], replicated, may hold values from -0.21875 to 0.21875
- step_proj: bfloat16 [2, 768, 24], P(None, None, 'head'), may hold values from -0.21875 to 0.21875
- conv_value: float32 [2, 4, 1536], P(None, None, 'head'), may hold values from -3 to 3
- conv_value_bias: float32 [2, 1536], P(None, 'head'), may hold values from -3 to 3
- conv_shared: float32 [2, 4, 256], replicated, may hold values from -3 to 3
- conv_shared_bias: float32 [2, 256], replicated, may hold values from -3 to 3
- step_bias: float32 [2, 24], P(None, 'head'), may hold values from -14 to -4
- decay_log: float32 [2, 24], P(None, 'head'), may hold values from -1 to 2
- skip_scale: float32 [2, 24], P(None, 'head'), may hold values from 0.5 to 2
- gate_gain: float32 [2, 1536], P(None, 'head'), may hold values from 0.5 to 1.5
- out_proj: bfloat16 [2, 1536, 768], P(None, 'head'), may hold values from -0.15625 to 0.15625
Outputs:
- hidden_out: float32 [2, 512, 768], P('batch', 'seq')
- hidden_grad: float32 [2, 512, 768], P('batch', 'seq')
- grad_norm_gain: float32 [2, 768], replicated
- grad_gate_proj: float32 [2, 768, 1536], P(None, ('seq', 'batch'), 'head')
- grad_value_proj: float32 [2, 768, 1536], P(None, ('seq', 'batch'), 'head')
- grad_shared_proj: float32 [2, 768, 256], P(None, ('seq', 'batch'))
- grad_step_proj: float32 [2, 768, 24], P(None, ('seq', 'batch'), 'head')
- grad_conv_value: float32 [2, 4, 1536], P(None, None, 'head')
- grad_conv_value_bias: float32 [2, 1536], P(None, 'head')
- grad_conv_shared: float32 [2, 4, 256], replicated
- grad_conv_shared_bias: float32 [2, 256], replicated
- grad_step_bias: float32 [2, 24], P(None, 'head')
- grad_decay_log: float32 [2, 24], P(None, 'head')
- grad_skip_scale: float32 [2, 24], P(None, 'head')
- grad_gate_gain: float32 [2, 1536], P(None, 'head')
- grad_out_proj: float32 [2, 1536, 768], P(None, 'head', ('seq', 'batch'))
All inputs are finite; a program needn't handle non-finite values.
Results may differ from a plain program's by a relative error of at most 0.012.
Values sent between devices are 32-bit elements; how exact they have to be, the bound alone decides.
A program may use at most 128 MiB of HBM per device.

v0:
```python
import jax
import jax.numpy as jnp
from jax import lax
from jax.sharding import PartitionSpec as P

GROUP = 128


epsilon = 1e-05
highest = lax.Precision.HIGHEST


def passed_along(value, axis, steps):
    count = lax.axis_size(axis)
    first, last = (max(0, -steps), min(count, count - steps))
    return lax.ppermute(value, axis, [(source, source + steps) for source in range(first, last)])


def prefix(x, axis, combine, identity, reverse):
    count, position = (lax.axis_size(axis), lax.axis_index(axis))
    everything = jax.tree.map(lambda part: lax.all_gather(part, axis), x)
    start = jax.tree.map(
        lambda part, zero: jnp.broadcast_to(jnp.asarray(zero, part.dtype), part.shape), x, identity
    )

    def turn(k, before):
        at = count - 1 - k if reverse else k
        reached = at > position if reverse else at < position
        new = combine(before, jax.tree.map(lambda part: part[at], everything))
        return jax.tree.map(lambda a, b: jnp.where(reached, a, b), new, before)

    return lax.fori_loop(0, count, turn, start)


def silu_slope(argument):
    sigmoid_value = jax.nn.sigmoid(argument)
    return sigmoid_value * (1.0 + argument * (1.0 - sigmoid_value))


def blocked(tensor, head_count):
    row_count = tensor.shape[0]
    return tensor.reshape(row_count // GROUP, GROUP, head_count, tensor.shape[1] // head_count)


def norm_input(hidden, norm_gain):
    return (
        hidden * lax.rsqrt(jnp.mean(hidden * hidden, axis=-1, keepdims=True) + epsilon) * norm_gain
    )


def ssd_front(
    ext_value,
    ext_shared,
    conv_value,
    conv_value_bias,
    conv_shared,
    conv_shared_bias,
    step_raw,
    step_bias,
    decay_log,
):
    row_count, head_count = step_raw.shape
    value_conv = conv_value_bias + jnp.zeros((row_count, ext_value.shape[1]), jnp.float32)
    shared_conv = conv_shared_bias + jnp.zeros((row_count, ext_shared.shape[1]), jnp.float32)
    for k in range(conv_value.shape[0]):
        value_conv = value_conv + conv_value[k] * ext_value[k : k + row_count]
        shared_conv = shared_conv + conv_shared[k] * ext_shared[k : k + row_count]
    values_act = jax.nn.silu(value_conv)
    shared_act = jax.nn.silu(shared_conv)
    state_width = shared_act.shape[1] // 2
    b_mat = shared_act[:, :state_width]
    c_mat = shared_act[:, state_width:]
    step_size = jax.nn.softplus(step_raw + step_bias)
    rate_values = -jnp.exp(decay_log) * step_size
    block_count = row_count // GROUP
    value_blocks = blocked(values_act, head_count)
    b_blocks = b_mat.reshape(block_count, GROUP, state_width)
    step_blocks = step_size.reshape(block_count, GROUP, head_count)
    cum_rates = jnp.cumsum(rate_values.reshape(block_count, GROUP, head_count), axis=1)
    to_end = jnp.exp(cum_rates[:, -1:, :] - cum_rates)
    weighted = value_blocks * (to_end * step_blocks)[..., None]
    summary = jnp.einsum("clhp,cln->chpn", weighted, b_blocks, precision=highest)
    block_decay = jnp.exp(cum_rates[:, -1, :])

    def fold_block(running, element):
        end_state, decay_total = running
        piece_state, piece_decay = element
        return (
            (piece_decay[:, None, None] * end_state + piece_state, decay_total * piece_decay),
            None,
        )

    start_pair = (jnp.zeros(summary.shape[1:], jnp.float32), jnp.ones((head_count,), jnp.float32))
    (end_state, decay_total), _ = lax.scan(fold_block, start_pair, (summary, block_decay))
    return (
        values_act,
        b_mat,
        c_mat,
        step_size,
        rate_values,
        summary,
        block_decay,
        end_state,
        decay_total,
    )


def ssd_output(
    values_act, b_mat, c_mat, step_size, rate_values, skip_scale, summary, block_decay, start_state
):
    row_count, head_count = step_size.shape
    block_count = row_count // GROUP
    state_width = b_mat.shape[1]
    value_blocks = blocked(values_act, head_count)
    b_blocks = b_mat.reshape(block_count, GROUP, state_width)
    c_blocks = c_mat.reshape(block_count, GROUP, state_width)
    step_heads = jnp.transpose(step_size.reshape(block_count, GROUP, head_count), (0, 2, 1))
    cum_rates = jnp.cumsum(
        jnp.transpose(rate_values.reshape(block_count, GROUP, head_count), (0, 2, 1)), axis=2
    )

    def advance(running, element):
        piece_state, piece_decay = element
        return (piece_decay[:, None, None] * running + piece_state, running)

    _, starts = lax.scan(advance, start_state, (summary, block_decay))
    scores = jnp.einsum("ctn,csn->cts", c_blocks, b_blocks, precision=highest)
    positions = jnp.arange(GROUP)
    causal = positions[:, None] >= positions[None, :]
    gap = cum_rates[:, :, :, None] - cum_rates[:, :, None, :]
    weights = jnp.where(causal, jnp.exp(jnp.where(causal, gap, 0.0)), 0.0)
    mixing = scores[:, None, :, :] * weights * step_heads[:, :, None, :]
    within_out = jnp.einsum("chts,cshp->cthp", mixing, value_blocks, precision=highest)
    carried = (
        jnp.einsum("ctn,chpn->cthp", c_blocks, starts, precision=highest)
        * jnp.exp(jnp.transpose(cum_rates, (0, 2, 1)))[..., None]
    )
    mixer_out = within_out + carried + skip_scale[None, None, :, None] * value_blocks
    return mixer_out.reshape(row_count, values_act.shape[1])


def combine(earlier, later):
    return (earlier[0] * later[0], later[1] + later[0][:, None, None] * earlier[1])


def layer_slice(stacked, layer_index):
    return tuple((tensor[layer_index] for tensor in stacked))


def layer_forward(hidden, layer_weights):
    (
        norm_gain,
        gate_proj,
        value_proj,
        shared_proj,
        step_proj,
        conv_value,
        conv_value_bias,
        conv_shared,
        conv_shared_bias,
        step_bias,
        decay_log,
        skip_scale,
        gate_gain,
        out_proj,
    ) = layer_weights
    normed_b = norm_input(hidden, norm_gain).astype(jnp.bfloat16)
    gate_pre = jnp.dot(normed_b, gate_proj, preferred_element_type=jnp.float32)
    value_pre = jnp.dot(normed_b, value_proj, preferred_element_type=jnp.float32)
    shared_pre = jnp.dot(normed_b, shared_proj, preferred_element_type=jnp.float32)
    step_raw = jnp.dot(normed_b, step_proj, preferred_element_type=jnp.float32)
    rim_rows = conv_value.shape[0] - 1
    prev_value, prev_shared = passed_along(
        (value_pre[-rim_rows:], shared_pre[-rim_rows:]), "seq", 1
    )
    ext_value = jnp.concatenate([prev_value, value_pre], axis=0)
    ext_shared = jnp.concatenate([prev_shared, shared_pre], axis=0)
    front_out, front_pull = jax.vjp(
        ssd_front,
        ext_value,
        ext_shared,
        conv_value,
        conv_value_bias,
        conv_shared,
        conv_shared_bias,
        step_raw,
        step_bias,
        decay_log,
    )
    end_state = front_out[7]
    decay_total = front_out[8]
    identity = (jnp.ones_like(decay_total), jnp.zeros_like(end_state))
    _, start_state = prefix((decay_total, end_state), "seq", combine, identity, False)
    mixer_out, output_pull = jax.vjp(
        ssd_output,
        front_out[0],
        front_out[1],
        front_out[2],
        front_out[3],
        front_out[4],
        skip_scale,
        front_out[5],
        front_out[6],
        start_state,
    )
    gated_out = mixer_out * jax.nn.silu(gate_pre)
    inner_width = gated_out.shape[1] * lax.axis_size("head")
    square_sum = lax.psum(jnp.sum(gated_out * gated_out, axis=-1), "head")
    inv_rms = lax.rsqrt(square_sum / inner_width + epsilon)[:, None]
    gated_b = (gated_out * inv_rms * gate_gain).astype(jnp.bfloat16)
    branch = lax.psum(jnp.dot(gated_b, out_proj, preferred_element_type=jnp.float32), "head")
    stored = (
        normed_b,
        gate_pre,
        front_pull,
        output_pull,
        mixer_out,
        gated_out,
        inv_rms,
        gated_b,
        hidden,
        start_state,
        decay_total,
    )
    return (hidden + branch, stored)


def layer_backward(d_hidden, stored, layer_weights):
    (
        norm_gain,
        gate_proj,
        value_proj,
        shared_proj,
        step_proj,
        conv_value,
        conv_value_bias,
        conv_shared,
        conv_shared_bias,
        step_bias,
        decay_log,
        skip_scale,
        gate_gain,
        out_proj,
    ) = layer_weights
    (
        normed_b,
        gate_pre,
        front_pull,
        output_pull,
        mixer_out,
        gated_out,
        inv_rms,
        gated_b,
        hidden,
        start_state,
        decay_total,
    ) = stored
    branch_b = d_hidden.astype(jnp.bfloat16)
    d_normalized = jnp.dot(branch_b, out_proj.T, preferred_element_type=jnp.float32)
    grad_out = jnp.dot(gated_b.T, branch_b, preferred_element_type=jnp.float32)
    grad_gain_gate = jnp.sum(d_normalized * gated_out * inv_rms, axis=0)
    scaled = d_normalized * gate_gain
    inner_width = gated_out.shape[1] * lax.axis_size("head")
    inner_sum = lax.psum(jnp.sum(scaled * gated_out, axis=-1), "head")
    inner_dot = (inner_sum / inner_width)[:, None]
    d_gated = inv_rms * scaled - gated_out * inv_rms * inv_rms * inv_rms * inner_dot
    d_mixer = d_gated * jax.nn.silu(gate_pre)
    d_gate_pre = d_gated * mixer_out * silu_slope(gate_pre)
    d_values, d_bmat, d_cmat, d_step, d_rates, grad_skip, d_summary, d_decay, d_start = output_pull(
        d_mixer
    )
    identity = (jnp.ones_like(decay_total), jnp.zeros_like(d_start))
    _, d_end = prefix((decay_total, d_start), "seq", combine, identity, True)
    d_total = jnp.sum(d_end * start_state, axis=(1, 2))
    pulled = front_pull(
        (d_values, d_bmat, d_cmat, d_step, d_rates, d_summary, d_decay, d_end, d_total)
    )
    (
        d_ext_value,
        d_ext_shared,
        grad_conv_v,
        grad_conv_vb,
        grad_conv_s,
        grad_conv_sb,
        d_step_raw,
        grad_step_bias,
        grad_decay,
    ) = pulled
    rim_rows = conv_value.shape[0] - 1
    from_value, from_shared = passed_along(
        (d_ext_value[:rim_rows], d_ext_shared[:rim_rows]), "seq", -1
    )
    d_value_pre = d_ext_value[rim_rows:].at[-rim_rows:].add(from_value)
    d_shared_pre = d_ext_shared[rim_rows:].at[-rim_rows:].add(from_shared)
    gate_b = d_gate_pre.astype(jnp.bfloat16)
    value_b = d_value_pre.astype(jnp.bfloat16)
    shared_b = d_shared_pre.astype(jnp.bfloat16)
    step_b = d_step_raw.astype(jnp.bfloat16)
    partial_normed = jnp.dot(gate_b, gate_proj.T, preferred_element_type=jnp.float32)
    partial_normed = partial_normed + jnp.dot(
        value_b, value_proj.T, preferred_element_type=jnp.float32
    )
    partial_normed = partial_normed + jnp.dot(
        shared_b, shared_proj.T, preferred_element_type=jnp.float32
    )
    partial_normed = partial_normed + jnp.dot(
        step_b, step_proj.T, preferred_element_type=jnp.float32
    )
    d_normed = lax.psum(partial_normed, "head")
    grad_gate = jnp.dot(normed_b.T, gate_b, preferred_element_type=jnp.float32)
    grad_value = jnp.dot(normed_b.T, value_b, preferred_element_type=jnp.float32)
    grad_shared = jnp.dot(normed_b.T, shared_b, preferred_element_type=jnp.float32)
    grad_step = jnp.dot(normed_b.T, step_b, preferred_element_type=jnp.float32)
    _, norm_pull = jax.vjp(norm_input, hidden, norm_gain)
    d_input, grad_norm = norm_pull(d_normed)
    return (
        d_hidden + d_input,
        (
            grad_norm,
            grad_gate,
            grad_value,
            grad_shared,
            grad_step,
            grad_conv_v,
            grad_conv_vb,
            grad_conv_s,
            grad_conv_sb,
            grad_step_bias,
            grad_decay,
            grad_skip,
            grad_gain_gate,
            grad_out,
        ),
    )


def reduce_grads(grads):
    gate_sum, value_sum, step_sum, out_sum, shared_part = (
        lax.psum_scatter(grads[1], ("seq", "batch"), scatter_dimension=1, tiled=True),
        lax.psum_scatter(grads[2], ("seq", "batch"), scatter_dimension=1, tiled=True),
        lax.psum_scatter(grads[4], ("seq", "batch"), scatter_dimension=1, tiled=True),
        lax.psum_scatter(grads[13], ("seq", "batch"), scatter_dimension=2, tiled=True),
        lax.psum_scatter(grads[3], ("seq", "batch"), scatter_dimension=1, tiled=True),
    )
    small_sums = lax.psum(
        (
            grads[0],
            grads[5],
            grads[6],
            grads[7],
            grads[8],
            grads[9],
            grads[10],
            grads[11],
            grads[12],
        ),
        ("seq", "batch"),
    )
    shared_sum, conv_shared_sum, conv_bias_sum = lax.psum(
        (shared_part, small_sums[3], small_sums[4]), "head"
    )
    return (
        small_sums[0],
        gate_sum,
        value_sum,
        shared_sum,
        step_sum,
        small_sums[1],
        small_sums[2],
        conv_shared_sum,
        conv_bias_sum,
        small_sums[5],
        small_sums[6],
        small_sums[7],
        small_sums[8],
        out_sum,
    )


def body(
    hidden_in,
    cotangent,
    norm_gain,
    gate_proj,
    value_proj,
    shared_proj,
    step_proj,
    conv_value,
    conv_value_bias,
    conv_shared,
    conv_shared_bias,
    step_bias,
    decay_log,
    skip_scale,
    gate_gain,
    out_proj,
):
    stacked = (
        norm_gain,
        gate_proj,
        value_proj,
        shared_proj,
        step_proj,
        conv_value,
        conv_value_bias,
        conv_shared,
        conv_shared_bias,
        step_bias,
        decay_log,
        skip_scale,
        gate_gain,
        out_proj,
    )
    layer_total = norm_gain.shape[0]
    hidden = hidden_in[0]
    stored_all = []
    for layer_index in range(layer_total):
        hidden, stored = layer_forward(hidden, layer_slice(stacked, layer_index))
        stored_all.append(stored)
    d_hidden = cotangent[0]
    raw_grads = [None] * layer_total
    reduced = [None] * layer_total
    for layer_index in reversed(range(layer_total)):
        d_hidden, raw_grads[layer_index] = layer_backward(
            d_hidden, stored_all[layer_index], layer_slice(stacked, layer_index)
        )
        reduced[layer_index] = reduce_grads(
            tuple((entry[None] for entry in raw_grads[layer_index]))
        )
    reduced_all = [jnp.concatenate([member[i] for member in reduced], axis=0) for i in range(14)]
    return (
        hidden[None],
        d_hidden[None],
        reduced_all[0],
        reduced_all[1],
        reduced_all[2],
        reduced_all[3],
        reduced_all[4],
        reduced_all[5],
        reduced_all[6],
        reduced_all[7],
        reduced_all[8],
        reduced_all[9],
        reduced_all[10],
        reduced_all[11],
        reduced_all[12],
        reduced_all[13],
    )


def solution(mesh):
    return jax.shard_map(
        body,
        mesh=mesh,
        in_specs=(
            P("batch", "seq", None),
            P("batch", "seq", None),
            P(),
            P(None, None, "head"),
            P(None, None, "head"),
            P(),
            P(None, None, "head"),
            P(None, None, "head"),
            P(None, "head"),
            P(),
            P(),
            P(None, "head"),
            P(None, "head"),
            P(None, "head"),
            P(None, "head"),
            P(None, "head", None),
        ),
        out_specs=(
            P("batch", "seq", None),
            P("batch", "seq", None),
            P(),
            P(None, ("seq", "batch"), "head"),
            P(None, ("seq", "batch"), "head"),
            P(None, ("seq", "batch"), None),
            P(None, ("seq", "batch"), "head"),
            P(None, None, "head"),
            P(None, "head"),
            P(),
            P(),
            P(None, "head"),
            P(None, "head"),
            P(None, "head"),
            P(None, "head"),
            P(None, "head", ("seq", "batch")),
        ),
        check_vma=False,
    )
```

profile of v0, /device:TPU:0, one launch (start us, length us, event | category | flops | bytes accessed | tf_op | source)
XLA Modules:
  0.0 768.8 jit_solution(7923201844809319494)
XLA Ops:
  11.8 5.0 collective-permute-start
  17.0 3.5 collective-permute-start.1
  24.6 9.1 %all-gather.1 = f32[4,1,6]{2,1,0:T(1,128)S(1)} all-gather(f32[1,1,6]{2,1,0:T(1,128)S(1)} %copy.173), channel_id=3, replica_groups=mesh['seq'=4,'head'=4,'batch'=2] {'seq'}, dimensions={0}, use_global_device_ids=true | all-gather | bytes 120 | tf_op jit(solution)/shard_map/all_gather | solution.py:21
  36.0 16.7 %all-gather = f32[24,64,128]{2,1,0:T(8,128)S(1)} all-gather(f32[6,64,128]{2,1,0:T(8,128)S(1)} %convolution_add_fusion.7), channel_id=2, replica_groups=mesh['seq'=4,'head'=4,'batch'=2] {'seq'}, dimensions={0}, use_global_device_ids=true | all-gather | bytes 983040 | tf_op jit(solution)/shard_map/all_gather | solution.py:21
  57.0 10.0 %psum.224 = f32[128]{0:T(128)S(1)} all-reduce(f32[128]{0:T(128)S(1)} %get-tuple-element.992), channel_id=1, replica_groups=mesh['seq'=4,'head'=4,'batch'=2] {'head'}, use_global_device_ids=true, to_apply=%region_6.8 | all-reduce | flops 128 | bytes 1024 | tf_op jit(solution)/shard_map/psum | solution.py:208
  68.2 41.3 %all-reduce.51.cloned.1.call-done = f32[128,768]{1,0:T(8,128)} async-done(((f32[128,768]{1,0:T(8,128)}), f32[128,768]{1,0:T(8,128)}) %all-reduce.51.cloned.1.call-update) | async-done | bytes 393232 | tf_op jit(solution)/shard_map/psum | solution.py:211
  115.8 3.4 collective-permute-start.2
  119.2 3.4 collective-permute-start.3
  123.0 9.0 %all-gather.3 = f32[4,1,6]{2,1,0:T(1,128)} all-gather(f32[1,1,6]{2,1,0:T(1,128)S(1)} %copy.183), channel_id=5, replica_groups=mesh['seq'=4,'head'=4,'batch'=2] {'seq'}, dimensions={0}, use_global_device_ids=true | all-gather | bytes 120 | tf_op jit(solution)/shard_map/all_gather | solution.py:21
  143.4 17.2 %all-gather.2 = f32[24,64,128]{2,1,0:T(8,128)} all-gather(f32[6,64,128]{2,1,0:T(8,128)S(1)} %convolution_add_fusion.6), channel_id=4, replica_groups=mesh['seq'=4,'head'=4,'batch'=2] {'seq'}, dimensions={0}, use_global_device_ids=true | all-gather | bytes 983040 | tf_op jit(solution)/shard_map/all_gather | solution.py:21
  160.6 8.9 %while.45 = (s32[]{:T(128)}, f32[6,64,128]{2,1,0:T(8,128)S(1)}, s32[]{:T(128)}, f32[4,6,64,128]{3,2,1,0:T(8,128)}, f32[4,6]{1,0:T(4,128)}, /*index=5*/s32[]{:T(128)}, s32[]{:T(128)}) while((s32[]{:T(128)}, f32[6,64,128]{2,1,0:T(8,128)S(1)}, s32[]{:T(128)}, f32[4,6,64,128]{3,2,1,0:T(8,128)}, f32[4,6]{1,0:T(4,128)}, ...), condition=%wide.region_12.14_spmd.clone, body=%wide.region_11.13_spmd.clone.sunk | while | flops 196612 | bytes 590009 | solution.py:32
  176.8 8.9 %psum.226 = f32[128]{0:T(128)S(1)} all-reduce(f32[128]{0:T(128)S(1)} %get-tuple-element.984), channel_id=1, replica_groups=mesh['seq'=4,'head'=4,'batch'=2] {'head'}, use_global_device_ids=true, to_apply=%region_14.16 | all-reduce | flops 128 | bytes 1024 | tf_op jit(solution)/shard_map/psum | solution.py:208
  188.2 8.7 %psum.228 = f32[128]{0:T(128)S(1)} all-reduce(f32[128]{0:T(128)S(1)} %get-tuple-element.865), channel_id=1, replica_groups=mesh['seq'=4,'head'=4,'batch'=2] {'head'}, use_global_device_ids=true, to_apply=%region_17.19 | all-reduce | flops 128 | bytes 1024 | tf_op jit(solution)/shard_map/psum | solution.py:264
  204.0 16.5 %all-gather.4 = f32[24,64,128]{2,1,0:T(8,128)} all-gather(f32[6,64,128]{2,1,0:T(8,128)S(1)} %convolution_add_fusion.5), channel_id=6, replica_groups=mesh['seq'=4,'head'=4,'batch'=2] {'seq'}, dimensions={0}, use_global_device_ids=true | all-gather | bytes 983040 | tf_op jit(solution)/shard_map/all_gather | solution.py:21
  220.5 6.9 while.46
  284.2 4.7 copy.209
  291.2 32.4 %all-reduce.53.cloned.1.call-done = f32[128,768]{1,0:T(8,128)} async-done(((f32[128,768]{1,0:T(8,128)}), f32[128,768]{1,0:T(8,128)}) %all-reduce.53.cloned.1.call-update) | async-done | bytes 393232 | tf_op jit(solution)/shard_map/psum | solution.py:309
  329.1 8.9 %psum.230 = f32[128]{0:T(128)S(1)} all-reduce(f32[128]{0:T(128)S(1)} %get-tuple-element.863), channel_id=1, replica_groups=mesh['seq'=4,'head'=4,'batch'=2] {'head'}, use_global_device_ids=true, to_apply=%region_35.37 | all-reduce | flops 128 | bytes 1024 | tf_op jit(solution)/shard_map/psum | solution.py:264
  348.5 19.2 %all-gather.5 = f32[24,64,128]{2,1,0:T(8,128)} all-gather(f32[6,64,128]{2,1,0:T(8,128)S(1)} %convolution_add_fusion.4), channel_id=7, replica_groups=mesh['seq'=4,'head'=4,'batch'=2] {'seq'}, dimensions={0}, use_global_device_ids=true | all-gather | bytes 983040 | tf_op jit(solution)/shard_map/all_gather | solution.py:21
  367.8 6.9 while.47
  382.8 3.1 collective-permute-done.7
  396.4 4.7 copy.208
  410.7 4.1 collective-permute-done.6
  424.2 30.1 %reduce-scatter.25.cloned.1.call-done = f32[96,6]{1,0:T(8,128)} async-done(((f32[768,6]{1,0:T(8,128)}), f32[96,6]{1,0:T(8,128)}) %reduce-scatter.25.cloned.1.call-update) | async-done | bytes 2320
  455.8 66.2 %all-reduce.55.cloned.1.call-done = (f32[1,384,768]{1,0,2:T(1,128)}, f32[1,384,768]{1,0,2:T(1,128)}) async-done(((f32[1,384,768]{1,0,2:T(1,128)}, f32[1,384,768]{1,0,2:T(1,128)}), (f32[1,384,768]{1,0,2:T(1,128)}, f32[1,384,768]{1,0,2:T(1,128)})) %all-reduce.55.cloned.1.call-update) | async-done | bytes 2359312
  524.2 32.0 %reduce-scatter.15.cloned.1.call-done = f32[1,96,384]{2,1,0:T(8,128)} async-done(((f32[1,768,384]{2,1,0:T(8,128)}), f32[1,96,384]{2,1,0:T(8,128)}) %reduce-scatter.15.cloned.1.call-update) | async-done | bytes 147472 | tf_op jit(solution)/shard_map/reduce_scatter | solution.py:339
  556.3 33.4 %reduce-scatter.13.cloned.1.call-done = f32[1,96,384]{2,1,0:T(8,128)} async-done(((f32[1,768,384]{2,1,0:T(8,128)}), f32[1,96,384]{2,1,0:T(8,128)}) %reduce-scatter.13.cloned.1.call-update) | async-done | bytes 147472 | tf_op jit(solution)/shard_map/reduce_scatter | solution.py:339
  591.4 31.6 %reduce-scatter.19.cloned.1.call-done = f32[1,96,384]{2,1,0:T(8,128)} async-done(((f32[1,768,384]{2,1,0:T(8,128)}), f32[1,96,384]{2,1,0:T(8,128)}) %reduce-scatter.19.cloned.1.call-update) | async-done | bytes 147472 | tf_op jit(solution)/shard_map/reduce_scatter | solution.py:340
  623.0 33.6 %reduce-scatter.17.cloned.1.call-done = f32[1,96,384]{2,1,0:T(8,128)} async-done(((f32[1,768,384]{2,1,0:T(8,128)}), f32[1,96,384]{2,1,0:T(8,128)}) %reduce-scatter.17.cloned.1.call-update) | async-done | bytes 147472 | tf_op jit(solution)/shard_map/reduce_scatter | solution.py:340
  658.3 51.9 %all-reduce.57.cloned.1.call-done = (f32[128,768]{1,0:T(8,128)}, f32[128,768]{1,0:T(8,128)}, f32[1,96,256]{2,1,0:T(8,128)}, f32[1,96,256]{2,1,0:T(8,128)}) async-done(((f32[128,768]{1,0:T(8,128)}, f32[128,768]{1,0:T(8,128)}, f32[1,96,256]{2,1,0:T(8,128)}, f32[1,96,256]{2,1,0:T(8,128)}), (f32[128,768]{1,0:T(8,128)}, f32[128,768]{1,0:T(8,128)}, f32[1,96,256]{2,1,0:T(8,128)}, ...) | async-done | bytes 983056 | tf_op jit(solution)/shard_map/psum | solution.py:211
  713.2 28.9 %all-reduce.42 = (f32[1,768]{1,0:T(1,128)S(1)}, f32[1,768]{1,0:T(1,128)S(1)}, f32[1,4,384]{2,1,0:T(4,128)S(1)}, f32[1,4,384]{2,1,0:T(4,128)S(1)}, f32[1,384]{1,0...) all-reduce(f32[1,768]{1,0:T(1,128)S(1)} %reshape.1095, ...), channel_id=1, replica_groups=mesh['seq'=4,'head'=4,'batch'=2] {'seq','batch'}, use_global_device_ids=true, to_apply=%region_55.57 | all-reduce | flops 8740 | bytes 69920 | tf_op jit(solution)/shard_map/psum | solution.py:345
  744.1 15.0 %all-reduce.44 = (f32[1,4,256]{2,1,0:T(4,128)S(1)}, f32[1,4,256]{2,1,0:T(4,128)S(1)}, f32[1,256]{1,0:T(1,128)S(1)}, f32[1,256]{1,0:T(1,128)S(1)}) all-reduce(f32[1,4,256]{2,1,0:T(4,128)S(1)} %get-tuple-element.946, f32[1,4,256]{2,1,0:T(4,128)S(1)} %get-tuple-element.947, ...), channel_id=1, replica_groups=mesh['seq'=4,'head'=4,'batch'=2] {'head'}, use_global_device_ids=true, to_apply=%region_91.93 | all-reduce | flops 2560 | bytes 20480 | tf_op jit(solution)/shard_map/psum | solution.py:359
  (709 shorter events, 198.4 us)
Async XLA Ops:
  7.2 102.2 %all-reduce.51.cloned.1.call-start = ((), (), s32[]{:S(2)}) async-start(), calls=%async_computation.8 | async-start | bytes 786432 | tf_op jit(solution)/shard_map/psum | solution.py:211
  9.2 100.2 %copy-start.155 = (f32[128]{0:T(128)}, f32[128]{0:T(128)S(1)}, u32[]{:S(2)}) copy-start(f32[128]{0:T(128)S(1)} %fusion.192) | copy-start | bytes 1540
  11.8 23.2 %collective-permute-start = (f32[3,384]{1,0:T(4,128)S(1)}, f32[3,384]{1,0:T(4,128)S(1)}, u32[]{:S(2)}, u32[]{:S(2)}) collective-permute-start(f32[3,384]{1,0:T(4,128)S(1)} %slice.416), channel_id=1, source_target_pairs={{0,8},{8,16},{16,24},{1,9},{9,17},{17,25},{2,10},{10,18},{18,26},{... | collective-permute-start | bytes 13832 | tf_op jit(solution)/shard_map/ppermute | solution.py:16
  17.0 17.0 %collective-permute-start.1 = (f32[3,256]{1,0:T(4,128)S(1)}, f32[3,256]{1,0:T(4,128)S(1)}, u32[]{:S(2)}, u32[]{:S(2)}) collective-permute-start(f32[3,256]{1,0:T(4,128)S(1)} %slice.421), channel_id=1, source_target_pairs={{0,8},{8,16},{16,24},{1,9},{9,17},{17,25},{2,10},{10,18},{18,26},{... | collective-permute-start | bytes 9224 | tf_op jit(solution)/shard_map/ppermute | solution.py:16
  21.0 91.0 %copy-start.79 = (bf16[1,768,6]{1,0,2:T(2,128)(2,1)}, bf16[1,768,6]{1,0,2:T(2,128)(2,1)S(1)}, u32[]{:S(2)}) copy-start(bf16[1,768,6]{1,0,2:T(2,128)(2,1)S(1)} %get-tuple-element.1017) | copy-start | bytes 27652
  22.4 116.3 %copy-start.97 = (f32[384]{0:T(512)}, f32[384]{0:T(512)S(1)}, u32[]{:S(2)}) copy-start(f32[384]{0:T(512)S(1)} %get-tuple-element.886) | copy-start | bytes 4612
  22.4 116.3 %copy-start.99 = (f32[384]{0:T(512)}, f32[384]{0:T(512)S(1)}, u32[]{:S(2)}) copy-start(f32[384]{0:T(512)S(1)} %get-tuple-element.887) | copy-start | bytes 4612
  22.4 116.3 %copy-start.100 = (f32[384]{0:T(512)}, f32[384]{0:T(512)S(1)}, u32[]{:S(2)}) copy-start(f32[384]{0:T(512)S(1)} %get-tuple-element.892) | copy-start | bytes 4612
  22.4 116.3 %copy-start.101 = (f32[384]{0:T(512)}, f32[384]{0:T(512)S(1)}, u32[]{:S(2)}) copy-start(f32[384]{0:T(512)S(1)} %get-tuple-element.893) | copy-start | bytes 4612
  23.1 113.8 %copy-start.129 = (f32[1,1,256]{2,1,0:T(1,128)}, f32[1,1,256]{2,1,0:T(1,128)S(1)}, u32[]{:S(2)}) copy-start(f32[1,1,256]{2,1,0:T(1,128)S(1)} %get-tuple-element.1021) | copy-start | bytes 3076
  24.6 42.4 %copy-start.74 = (f32[384]{0:T(512)}, f32[384]{0:T(512)S(1)}, u32[]{:S(2)}) copy-start(f32[384]{0:T(512)S(1)} %get-tuple-element.897) | copy-start | bytes 4612
  56.9 52.5 %copy-start = (f32[1,128,768]{2,1,0:T(8,128)S(1)}, f32[1,128,768]{2,1,0:T(8,128)}, u32[]{:S(2)}) copy-start(f32[1,128,768]{2,1,0:T(8,128)} %param.33) | copy-start | bytes 1179652
  67.0 43.6 %copy-start.133 = (f32[128]{0:T(128)}, f32[128]{0:T(128)S(1)}, u32[]{:S(2)}) copy-start(f32[128]{0:T(128)S(1)} %add_rsqrt_fusion.1) | copy-start | bytes 1540
  68.1 255.5 %all-reduce.53.cloned.1.call-start = ((), (), s32[]{:S(2)}) async-start(), calls=%async_computation.9 | async-start | bytes 786432 | tf_op jit(solution)/shard_map/psum | solution.py:309
  115.8 22.8 %collective-permute-start.2 = (f32[3,384]{1,0:T(4,128)S(1)}, f32[3,384]{1,0:T(4,128)S(1)}, u32[]{:S(2)}, u32[]{:S(2)}) collective-permute-start(f32[3,384]{1,0:T(4,128)S(1)} %slice.428), channel_id=1, source_target_pairs={{0,8},{8,16},{16,24},{1,9},{9,17},{17,25},{2,10},{10,18},{18,26},{... | collective-permute-start | bytes 13832 | tf_op jit(solution)/shard_map/ppermute | solution.py:16
  119.2 17.6 %collective-permute-start.3 = (f32[3,256]{1,0:T(4,128)S(1)}, f32[3,256]{1,0:T(4,128)S(1)}, u32[]{:S(2)}, u32[]{:S(2)}) collective-permute-start(f32[3,256]{1,0:T(4,128)S(1)} %slice.433), channel_id=1, source_target_pairs={{0,8},{8,16},{16,24},{1,9},{9,17},{17,25},{2,10},{10,18},{18,26},{... | collective-permute-start | bytes 9224 | tf_op jit(solution)/shard_map/ppermute | solution.py:16
  266.5 5.6 collective-permute-start.5
  269.3 6.5 collective-permute-start.4
  280.6 138.9 %reduce-scatter.27.cloned.1.call-start = ((), (), s32[]{:S(2)}) async-start(), calls=%async_computation.17 | async-start | bytes 442368
  289.9 133.8 %reduce-scatter.23.cloned.1.call-start = ((), (), s32[]{:S(2)}) async-start(), calls=%async_computation.15 | async-start | bytes 884736 | tf_op jit(solution)/shard_map/reduce_scatter | solution.py:343
  291.2 132.5 %reduce-scatter.21.cloned.1.call-start = ((), (), s32[]{:S(2)}) async-start(), calls=%async_computation.14 | async-start | bytes 884736 | tf_op jit(solution)/shard_map/reduce_scatter | solution.py:343
  380.1 5.8 collective-permute-start.7
  388.1 66.2 %reduce-scatter.25.cloned.1.call-start = ((), (), s32[]{:S(2)}) async-start(), calls=%async_computation.16 | async-start | bytes 442368
  394.0 128.0 %all-reduce.55.cloned.1.call-start = ((), (), s32[]{:S(2)}) async-start(), calls=%async_computation.18 | async-start | bytes 4718592
  401.1 155.1 %reduce-scatter.15.cloned.1.call-start = ((), (), s32[]{:S(2)}) async-start(), calls=%async_computation.11 | async-start | bytes 1327104 | tf_op jit(solution)/shard_map/reduce_scatter | solution.py:339
  403.4 186.3 %reduce-scatter.13.cloned.1.call-start = ((), (), s32[]{:S(2)}) async-start(), calls=%async_computation.10 | async-start | bytes 1327104 | tf_op jit(solution)/shard_map/reduce_scatter | solution.py:339
  404.9 218.1 %reduce-scatter.19.cloned.1.call-start = ((), (), s32[]{:S(2)}) async-start(), calls=%async_computation.13 | async-start | bytes 1327104 | tf_op jit(solution)/shard_map/reduce_scatter | solution.py:340
  406.4 250.2 %reduce-scatter.17.cloned.1.call-start = ((), (), s32[]{:S(2)}) async-start(), calls=%async_computation.12 | async-start | bytes 1327104 | tf_op jit(solution)/shard_map/reduce_scatter | solution.py:340
  409.3 5.6 collective-permute-start.6
  416.6 293.6 %all-reduce.57.cloned.1.call-start = ((), (), s32[]{:S(2)}) async-start(), calls=%async_computation.19 | async-start | bytes 1966080 | tf_op jit(solution)/shard_map/psum | solution.py:211
  524.2 187.8 %copy-start.156 = (f32[128]{0:T(128)S(1)}, f32[128]{0:T(128)}, u32[]{:S(2)}) copy-start(f32[128]{0:T(128)} %copy-done.155) | copy-start | bytes 1540
  591.4 120.9 %copy-start.194 = (f32[128]{0:T(128)S(1)}, f32[128]{0:T(128)}, u32[]{:S(2)}) copy-start(f32[128]{0:T(128)} %copy-done.193) | copy-start | bytes 1540
  (189 other events, 1481.5 us)
Sparse Core Ops, SparseCore 0:
  68.2 41.1 all-reduce.50
  280.7 42.9 all-reduce.52
  326.5 31.2 reduce-scatter.26
  360.0 30.4 reduce-scatter.22
  392.6 30.3 reduce-scatter.20
  425.1 29.1 reduce-scatter.24
  456.8 65.2 all-reduce.54
  524.3 31.8 reduce-scatter.14
  558.5 31.0 reduce-scatter.12
  591.8 31.1 reduce-scatter.18
  625.3 31.2 reduce-scatter.16
  660.4 49.7 all-reduce.56
where the time goes:
time: 772 us; the launch traced here: 769 us
  waiting for transfers between devices  363 us (47%)
  blocking collectives  168 us (22%)
  other arithmetic  73.3 us (9%)
  matrix products  65.2 us (8%)
  local copies, waits for them, and re-layouts  59.5 us (8%)
  starting transfers between devices  21 us (3%)
  between operations  17.9 us (2%)
    unnamed x15, waiting for transfers between devices  96.5 us
    psum x2, waiting for transfers between devices, layer_forward(): lax.psum(jnp.dot(gated_b, out_proj, preferred_element_type=jnp.float32),...  93.2 us
    all_gather x6, blocking collectives, prefix(): everything = jax.tree.map(lambda part: lax.all_gather(part, axis), x)  87.8 us
    reduce_scatter x2, waiting for transfers between devices, reduce_grads(): lax.psum_scatter(grads[1], ('seq', 'batch'), scatter_dimension=1, tiled=T...  65.4 us
    reduce_scatter x2, waiting for transfers between devices, reduce_grads(): lax.psum_scatter(grads[2], ('seq', 'batch'), scatter_dimension=1, tiled=T...  65.2 us
    psum x1, waiting for transfers between devices, layer_backward(): d_normed = lax.psum(partial_normed, 'head')  32.4 us
    psum x1, blocking collectives, reduce_grads(): lax.psum((grads[0], grads[5], grads[6], grads[7], grads[8], grads[9], gra...  28.9 us
    ppermute x8, starting transfers between devices, passed_along(): lax.ppermute(value, axis, [(source, source + steps) for source in range(f...  20.5 us
  transfers between devices with their start and end apart: 20, of which 13 were waited for; matrix products, arithmetic and copies ran while one was open for 12% of the time, Pallas kernels for 0%

commit v1 on v0

v1 whole, which is shorter than its diff:
```python
import functools

import jax
import jax.numpy as jnp
from jax import lax
from jax.experimental import pallas as pl
from jax.experimental.pallas import tpu as pltpu
from jax.sharding import PartitionSpec as P

epsilon = 1e-05
highest = lax.Precision.HIGHEST
MESH_ID = pl.DeviceIdType.MESH
VMEM = pl.BlockSpec(memory_space=pltpu.VMEM)


def flat_index(axes):
    index = 0
    for axis, size in axes:
        index = index * size + lax.axis_index(axis)
    return index


def device_of(axes, flat):
    if len(axes) == 1:
        return {axes[0][0]: flat}
    (outer, _), (inner, size) = axes
    return {outer: flat // size, inner: flat % size}


def greet(devices):
    barrier = pltpu.get_barrier_semaphore()
    for device in devices:
        pl.semaphore_signal(barrier, inc=1, device_id=device, device_id_type=MESH_ID)
    return barrier


def all_reduce_kernel(axes, count, x_ref, o_ref, recv, send1, recv1, send2, recv2):
    me = flat_index(axes)
    peers = [lax.rem(me + d, count) for d in range(1, count)]
    barrier = greet([device_of(axes, peer) for peer in peers])
    pl.semaphore_wait(barrier, count - 1)
    first = []
    for d, peer in enumerate(peers):
        copy = pltpu.make_async_remote_copy(
            src_ref=x_ref.at[peer],
            dst_ref=recv.at[d],
            send_sem=send1.at[d],
            recv_sem=recv1.at[d],
            device_id=device_of(axes, peer),
            device_id_type=MESH_ID,
        )
        copy.start()
        first.append(copy)
    total = x_ref[me]
    for d, copy in enumerate(first):
        copy.wait_recv()
        total = total + recv[d]
    o_ref[me] = total
    second = []
    for d, peer in enumerate(peers):
        copy = pltpu.make_async_remote_copy(
            src_ref=o_ref.at[me],
            dst_ref=o_ref.at[me],
            send_sem=send2.at[d],
            recv_sem=recv2.at[d],
            device_id=device_of(axes, peer),
            device_id_type=MESH_ID,
        )
        copy.start()
        second.append(copy)
    for copy in first:
        copy.wait_send()
    for copy in second:
        copy.wait()


def all_reduce(x, axes, collective_id):
    axes = [(axis, lax.axis_size(axis)) for axis in axes]
    count = 1
    for _, size in axes:
        count *= size
    rows, width = x.shape
    part = (rows // count, width)
    out = pl.pallas_call(
        functools.partial(all_reduce_kernel, axes, count),
        out_shape=jax.ShapeDtypeStruct((count,) + part, jnp.float32),
        in_specs=[VMEM],
        out_specs=VMEM,
        scratch_shapes=[pltpu.VMEM((count - 1,) + part, jnp.float32)]
        + [pltpu.SemaphoreType.DMA((count - 1,))] * 4,
        compiler_params=pltpu.CompilerParams(
            collective_id=collective_id, has_side_effects=True
        ),
    )(x.reshape((count,) + part))
    return out.reshape(rows, width)


def placed(shapes, rows):
    pieces, at = [], 0
    for number, (height, _) in enumerate(shapes):
        begin = 0
        while begin < height:
            peer, inside = at // rows, at % rows
            take = min(height - begin, rows - inside)
            pieces.append((number, begin, take, peer, inside))
            begin, at = begin + take, at + take
    return pieces


def reduce_many_kernel(axes, count, shapes, outs, *refs):
    number = len(shapes)
    inputs, refs = refs[:number], refs[number:]
    outputs, refs = refs[: len(outs)], refs[len(outs) :]
    packed, total, *rest = refs
    pieces = placed(shapes, packed.shape[1])
    packed[...] = jnp.zeros_like(packed)
    for i, begin, take, peer, inside in pieces:
        packed[peer, inside : inside + take, : shapes[i][1]] = inputs[i][begin : begin + take, :]
    all_reduce_kernel(axes, count, packed, total, *rest)
    target = {}
    for o, members in enumerate(outs):
        for layer, i in enumerate(members):
            target[i] = (o, layer)
    for i, begin, take, peer, inside in pieces:
        o, layer = target[i]
        value = total[peer, inside : inside + take, : shapes[i][1]]
        if len(outputs[o].shape) == 3:
            outputs[o][layer, begin : begin + take, :] = value
        else:
            outputs[o][layer : layer + 1, :] = value


def reduce_many(groups, axes, collective_id):
    axes = [(axis, lax.axis_size(axis)) for axis in axes]
    count = 1
    for _, size in axes:
        count *= size
    arrays, outs, out_shapes = [], [], []
    for group in groups:
        outs.append(list(range(len(arrays), len(arrays) + len(group))))
        arrays += [array.reshape((-1, array.shape[-1])) for array in group]
        out_shapes.append(jax.ShapeDtypeStruct((len(group),) + group[0].shape, jnp.float32))
    shapes = [array.shape for array in arrays]
    height = sum(shape[0] for shape in shapes)
    rows = -(-height // (8 * count)) * 8
    part = (rows, -(-max(shape[1] for shape in shapes) // 128) * 128)
    return pl.pallas_call(
        functools.partial(reduce_many_kernel, axes, count, shapes, outs),
        out_shape=out_shapes,
        in_specs=[VMEM] * len(arrays),
        out_specs=[VMEM] * len(out_shapes),
        scratch_shapes=[pltpu.VMEM((count,) + part, jnp.float32)] * 2
        + [pltpu.VMEM((count - 1,) + part, jnp.float32)]
        + [pltpu.SemaphoreType.DMA((count - 1,))] * 4,
        compiler_params=pltpu.CompilerParams(
            collective_id=collective_id, has_side_effects=True
        ),
    )(*arrays)


def chain_kernel(count, step, decay_ref, end_ref, start_ref, held, send, recv):
    me = lax.axis_index("seq")
    first, last = (0, count - 1) if step == 1 else (count - 1, 0)
    after = lax.rem(me + step + count, count)
    before = lax.rem(me - step + count, count)
    barrier = pltpu.get_barrier_semaphore()

    @pl.when(me != first)
    def _():
        pl.semaphore_signal(barrier, inc=1, device_id={"seq": before}, device_id_type=MESH_ID)

    @pl.when(me != last)
    def _():
        pl.semaphore_wait(barrier, 1)

    copies = [
        pltpu.make_async_remote_copy(
            src_ref=held.at[h],
            dst_ref=start_ref.at[h],
            send_sem=send.at[h],
            recv_sem=recv.at[h],
            device_id={"seq": after},
            device_id_type=MESH_ID,
        )
        for h in range(end_ref.shape[0])
    ]
    for h, copy in enumerate(copies):

        @pl.when(me == first)
        def _():
            start_ref[h] = jnp.zeros_like(start_ref[h])
            held[h] = end_ref[h]

        @pl.when(me != first)
        def _():
            copy.wait_recv()
            held[h] = decay_ref[h] * start_ref[h] + end_ref[h]

        @pl.when(me != last)
        def _():
            copy.start()

    @pl.when(me != last)
    def _():
        for copy in copies:
            copy.wait_send()


def chain(decay, end, step, collective_id):
    count = lax.axis_size("seq")
    heads = end.shape[0]
    return pl.pallas_call(
        functools.partial(chain_kernel, count, step),
        out_shape=jax.ShapeDtypeStruct(end.shape, jnp.float32),
        in_specs=[VMEM, VMEM],
        out_specs=VMEM,
        scratch_shapes=[pltpu.VMEM(end.shape, jnp.float32)]
        + [pltpu.SemaphoreType.DMA((heads,))] * 2,
        compiler_params=pltpu.CompilerParams(
            collective_id=collective_id, has_side_effects=True
        ),
    )(jnp.broadcast_to(decay[:, None, None], (heads, 1, end.shape[2])), end)


def shift_kernel(count, step, x_ref, o_ref, send, recv):
    me = lax.axis_index("seq")
    first, last = (0, count - 1) if step == 1 else (count - 1, 0)
    after = lax.rem(me + step + count, count)
    before = lax.rem(me - step + count, count)
    barrier = pltpu.get_barrier_semaphore()

    @pl.when(me != first)
    def _():
        pl.semaphore_signal(barrier, inc=1, device_id={"seq": before}, device_id_type=MESH_ID)

    copy = pltpu.make_async_remote_copy(
        src_ref=x_ref,
        dst_ref=o_ref,
        send_sem=send,
        recv_sem=recv,
        device_id={"seq": after},
        device_id_type=MESH_ID,
    )

    @pl.when(me != last)
    def _():
        pl.semaphore_wait(barrier, 1)
        copy.start()

    @pl.when(me == first)
    def _():
        o_ref[...] = jnp.zeros_like(o_ref)

    @pl.when(me != first)
    def _():
        copy.wait_recv()

    @pl.when(me != last)
    def _():
        copy.wait_send()


def shift(x, step, collective_id):
    return pl.pallas_call(
        functools.partial(shift_kernel, lax.axis_size("seq"), step),
        out_shape=jax.ShapeDtypeStruct(x.shape, jnp.float32),
        in_specs=[VMEM],
        out_specs=VMEM,
        scratch_shapes=[pltpu.SemaphoreType.DMA] * 2,
        compiler_params=pltpu.CompilerParams(
            collective_id=collective_id, has_side_effects=True
        ),
    )(x)


def scatter_kernel(count, pairs, number, cuts, *refs):
    inputs, refs = refs[:number], refs[number:]
    outputs, refs = refs[: len(cuts)], refs[len(cuts) :]
    from_core, refs = refs[:number], refs[number:]
    partial, refs = refs[:number], refs[number:]
    from_left, refs = refs[:number], refs[number:]
    from_right, refs = refs[:number], refs[number:]
    core_send, core_recv, right_send, right_recv, left_send, left_recv = refs
    me, core = lax.axis_index("seq"), lax.axis_index("batch")
    others = [lax.rem(core + d, pairs) for d in range(1, pairs)]
    barrier = greet([{"batch": other} for other in others])
    right, left = lax.rem(me + 1, count), lax.rem(me + count - 1, count)

    @pl.when(me > 0)
    def _():
        pl.semaphore_signal(barrier, inc=1, device_id={"seq": left}, device_id_type=MESH_ID)

    @pl.when(me < count - 1)
    def _():
        pl.semaphore_signal(barrier, inc=1, device_id={"seq": right}, device_id_type=MESH_ID)

    edges = jnp.where(me > 0, 1, 0) + jnp.where(me < count - 1, 1, 0)
    pl.semaphore_wait(barrier, pairs - 1 + edges)

    order = []
    for k in range((count + 1) // 2):
        order.append(k)
        if count - 1 - k != k:
            order.append(count - 1 - k)
    across = {}
    for s in order:
        for i in range(number):
            for d, other in enumerate(others):
                across[i, s, d] = pltpu.make_async_remote_copy(
                    src_ref=inputs[i].at[s, other],
                    dst_ref=from_core[i].at[d, s],
                    send_sem=core_send.at[i, d, s],
                    recv_sem=core_recv.at[i, d, s],
                    device_id={"batch": other},
                    device_id_type=MESH_ID,
                )
                across[i, s, d].start()

    def along(i, s, buffer, sends, recvs, target):
        return pltpu.make_async_remote_copy(
            src_ref=partial[i].at[s],
            dst_ref=buffer[i].at[s],
            send_sem=sends.at[i, s],
            recv_sem=recvs.at[i, s],
            device_id={"seq": target},
            device_id_type=MESH_ID,
        )

    rightward = {
        (i, s): along(i, s, from_left, right_send, right_recv, right)
        for i in range(number)
        for s in range(1, count)
    }
    leftward = {
        (i, s): along(i, s, from_right, left_send, left_recv, left)
        for i in range(number)
        for s in range(count - 1)
    }
    done = set()

    def prepare(i, s):
        if (i, s) in done:
            return
        done.add((i, s))
        total = inputs[i][s, core]
        for d in range(len(others)):
            across[i, s, d].wait_recv()
            total = total + from_core[i][d, s]
        partial[i][s] = total

    def go_right(i, s, when):
        @pl.when(jnp.logical_and(when, me < s))
        def _():
            @pl.when(me > 0)
            def _():
                rightward[i, s].wait_recv()
                partial[i][s] = partial[i][s] + from_left[i][s]

            rightward[i, s].start()

    def go_left(i, s):
        @pl.when(me > s)
        def _():
            @pl.when(me < count - 1)
            def _():
                leftward[i, s].wait_recv()
                partial[i][s] = partial[i][s] + from_right[i][s]

            leftward[i, s].start()

    early = 2 * me < count
    for k in range(count - 1):
        for i in range(number):
            prepare(i, count - 1 - k)
            prepare(i, k)
            go_right(i, count - 1 - k, early)
            go_left(i, k)
            go_right(i, count - 1 - k, jnp.logical_not(early))
    for s in range(count):
        for i in range(number):
            prepare(i, s)

    for i in range(number):
        for s in range(count):

            @pl.when(me == s)
            def _():
                total = partial[i][s]

                def store(value):
                    for o, (kind, low, high) in enumerate(cuts):
                        if i % 2 == kind:
                            outputs[o][i // 2] = value[:, low:high]

                if s > 0:
                    rightward[i, s].wait_recv()
                    total = total + from_left[i][s]
                if s < count - 1:
                    leftward[i, s].wait_recv()
                    total = total + from_right[i][s]
                store(total)

    for copy in across.values():
        copy.wait_send()
    for (i, s), copy in rightward.items():

        @pl.when(me < s)
        def _():
            copy.wait_send()

    for (i, s), copy in leftward.items():

        @pl.when(me > s)
        def _():
            copy.wait_send()


def scatter_sum(grads, cuts, collective_id):
    count, pairs = lax.axis_size("seq"), lax.axis_size("batch")
    number = len(grads)
    parts = [(grad.shape[0] // (count * pairs), grad.shape[1]) for grad in grads]
    return pl.pallas_call(
        functools.partial(scatter_kernel, count, pairs, number, cuts),
        out_shape=[
            jax.ShapeDtypeStruct((number // 2, parts[kind][0], high - low), jnp.float32)
            for kind, low, high in cuts
        ],
        in_specs=[VMEM] * number,
        out_specs=[VMEM] * len(cuts),
        scratch_shapes=[pltpu.VMEM((pairs - 1, count) + part, jnp.float32) for part in parts]
        + [pltpu.VMEM((count,) + part, jnp.float32) for part in parts] * 3
        + [pltpu.SemaphoreType.DMA((number, pairs - 1, count))] * 2
        + [pltpu.SemaphoreType.DMA((number, count))] * 4,
        compiler_params=pltpu.CompilerParams(
            collective_id=collective_id, has_side_effects=True, vmem_limit_bytes=60 * 1024 * 1024
        ),
    )(*[grad.reshape((count, pairs) + part) for grad, part in zip(grads, parts)])


def silu_slope(argument):
    sigmoid_value = jax.nn.sigmoid(argument)
    return sigmoid_value * (1.0 + argument * (1.0 - sigmoid_value))


def norm_input(hidden, norm_gain):
    return (
        hidden * lax.rsqrt(jnp.mean(hidden * hidden, axis=-1, keepdims=True) + epsilon) * norm_gain
    )


def spread(per_head, width):
    heads = per_head.shape[-1]
    owner = jnp.arange(width) // (width // heads)
    table = (jnp.arange(heads)[:, None] == owner[None, :]).astype(jnp.float32)
    return jnp.dot(per_head, table, precision=highest)


def ssd_front(
    ext_value,
    ext_shared,
    conv_value,
    conv_value_bias,
    conv_shared,
    conv_shared_bias,
    step_raw,
    step_bias,
    decay_log,
):
    row_count, head_count = step_raw.shape
    value_conv, shared_conv = conv_value_bias, conv_shared_bias
    for k in range(conv_value.shape[0]):
        value_conv = value_conv + conv_value[k] * ext_value[k : k + row_count]
        shared_conv = shared_conv + conv_shared[k] * ext_shared[k : k + row_count]
    values = jax.nn.silu(value_conv)
    shared_act = jax.nn.silu(shared_conv)
    state_width = shared_act.shape[1] // 2
    b_mat = shared_act[:, :state_width]
    c_mat = shared_act[:, state_width:]
    step = jax.nn.softplus(step_raw + step_bias)
    rate = -jnp.exp(decay_log) * step
    positions = jnp.arange(row_count)
    causal = (positions[:, None] >= positions[None, :]).astype(jnp.float32)
    cum = jnp.dot(causal, rate, precision=highest)
    to_end = jnp.exp(cum[-1:] - cum)
    weighted = values * spread(to_end * step, values.shape[1])
    end_state = lax.dot_general(weighted, b_mat, (((0,), (0,)), ((), ())))
    return values, b_mat, c_mat, step, cum, end_state, jnp.exp(cum[-1])


def ssd_output(values, b_mat, c_mat, step, cum, skip_scale, start_state):
    row_count, head_count = step.shape
    width = values.shape[1]
    scores = lax.dot_general(c_mat, b_mat, (((1,), (1,)), ((), ())))
    positions = jnp.arange(row_count)
    causal = positions[:, None] >= positions[None, :]
    cum_heads = cum.T
    gap = cum_heads[:, :, None] - cum_heads[:, None, :]
    weights = jnp.where(causal, jnp.exp(jnp.where(causal, gap, 0.0)), 0.0)
    mixing = scores[None] * weights * step.T[:, None, :]
    within = jnp.einsum("hts,shp->thp", mixing, values.reshape(row_count, head_count, -1))
    carried = lax.dot_general(c_mat, start_state, (((1,), (1,)), ((), ())))
    carried = carried * spread(jnp.exp(cum), width)
    skipped = spread(skip_scale[None], width) * values
    return within.reshape(row_count, width) + carried + skipped


def layer_forward(hidden, weights):
    (norm_gain, wide_proj, conv_v, conv_vb, conv_s, conv_sb, step_bias, decay_log) = weights[:8]
    (skip_scale, gate_gain, out_proj) = weights[8:]
    inner, shared = conv_v.shape[1], conv_s.shape[1]
    heads = step_bias.shape[0]
    normed_b = norm_input(hidden, norm_gain).astype(jnp.bfloat16)
    wide = jnp.dot(normed_b, wide_proj, preferred_element_type=jnp.float32)
    gate_pre = wide[:, :inner]
    mixed = wide[:, inner : 2 * inner + shared]
    step_raw = wide[:, 2 * inner + shared :]
    rim = conv_v.shape[0] - 1
    before = shift(mixed[-8:], 1, 1)[-rim:]
    ext = jnp.concatenate([before, mixed], axis=0)
    front_out, front_pull = jax.vjp(
        ssd_front,
        ext[:, :inner],
        ext[:, inner:],
        conv_v,
        conv_vb,
        conv_s,
        conv_sb,
        step_raw,
        step_bias,
        decay_log,
    )
    values, b_mat, c_mat, step, cum, end_state, decay_total = front_out
    states = (heads, inner // heads, end_state.shape[1])
    start_state = chain(decay_total, end_state.reshape(states), 1, 2).reshape(end_state.shape)
    mixer_out, output_pull = jax.vjp(
        ssd_output, values, b_mat, c_mat, step, cum, skip_scale, start_state
    )
    gated = mixer_out * jax.nn.silu(gate_pre)
    branch = jnp.dot(
        (gated * gate_gain).astype(jnp.bfloat16), out_proj, preferred_element_type=jnp.float32
    )
    square = jnp.sum(gated * gated, axis=-1, keepdims=True)
    square = jnp.broadcast_to(square, (square.shape[0], 128))
    width = branch.shape[1]
    both = all_reduce(jnp.concatenate([branch, square], axis=1), ["head"], 3)
    branch = both[:, :width]
    inner_width = inner * lax.axis_size("head")
    inv_rms = lax.rsqrt(both[:, width : width + 1] / inner_width + epsilon)
    stored = (
        normed_b,
        gate_pre,
        front_pull,
        output_pull,
        mixer_out,
        gated,
        inv_rms,
        branch,
        hidden,
        start_state,
        decay_total,
    )
    return hidden + branch * inv_rms, stored


def layer_backward(d_hidden, stored, weights):
    (norm_gain, wide_proj, conv_v, conv_vb, conv_s, conv_sb, step_bias, decay_log) = weights[:8]
    (skip_scale, gate_gain, out_proj) = weights[8:]
    (
        normed_b,
        gate_pre,
        front_pull,
        output_pull,
        mixer_out,
        gated,
        inv_rms,
        branch,
        hidden,
        start_state,
        decay_total,
    ) = stored
    inner, shared = conv_v.shape[1], conv_s.shape[1]
    heads = step_bias.shape[0]
    g_b = d_hidden.astype(jnp.bfloat16)
    d_norm = lax.dot_general(
        g_b, out_proj, (((1,), (1,)), ((), ())), preferred_element_type=jnp.float32
    )
    gated_b = (gated * inv_rms * gate_gain).astype(jnp.bfloat16)
    grad_out = lax.dot_general(
        g_b, gated_b, (((0,), (0,)), ((), ())), preferred_element_type=jnp.float32
    )
    grad_gain_gate = jnp.sum(d_norm * gated * inv_rms, axis=0)
    scaled = d_norm * gate_gain
    inner_width = inner * lax.axis_size("head")
    inner_sum = jnp.sum(g_b.astype(jnp.float32) * branch, axis=-1, keepdims=True)
    inner_dot = inner_sum / inner_width
    d_gated = inv_rms * scaled - gated * (inv_rms * inv_rms * inv_rms * inner_dot)
    d_mixer = d_gated * jax.nn.silu(gate_pre)
    d_gate_pre = d_gated * mixer_out * silu_slope(gate_pre)
    d_values, d_b, d_c, d_step, d_cum, grad_skip, d_start = output_pull(d_mixer)
    states = (heads, inner // heads, d_start.shape[1])
    d_end = chain(decay_total, d_start.reshape(states), -1, 4)
    d_total = jnp.sum(d_end * start_state.reshape(states), axis=(1, 2))
    pulled = front_pull((d_values, d_b, d_c, d_step, d_cum, d_end.reshape(d_start.shape), d_total))
    d_ext_value, d_ext_shared, g_cv, g_cvb, g_cs, g_csb, d_step_raw, g_sb, g_decay = pulled
    rim = conv_v.shape[0] - 1
    d_ext = jnp.concatenate([d_ext_value, d_ext_shared], axis=1)
    after = shift(d_ext[:8], -1, 5)
    after = jnp.concatenate([jnp.zeros_like(d_ext[2 * rim :]), after[:rim]], axis=0)
    d_mixed = d_ext[rim:] + after
    step_b = d_step_raw.astype(jnp.bfloat16)
    projected_b = jnp.concatenate(
        [d_gate_pre.astype(jnp.bfloat16), d_mixed.astype(jnp.bfloat16)], axis=1
    )
    d_wide = jnp.concatenate([projected_b, step_b], axis=1)
    partial_normed = lax.dot_general(
        d_wide, wide_proj, (((1,), (1,)), ((), ())), preferred_element_type=jnp.float32
    )
    d_normed = all_reduce(partial_normed, ["head"], 6)
    grad_wide = lax.dot_general(
        normed_b, projected_b, (((0,), (0,)), ((), ())), preferred_element_type=jnp.float32
    )
    grad_step = lax.dot_general(
        step_b, normed_b, (((0,), (0,)), ((), ())), preferred_element_type=jnp.float32
    )
    _, norm_pull = jax.vjp(norm_input, hidden, norm_gain)
    d_input, grad_norm = norm_pull(d_normed)
    small = (grad_norm, g_cv, g_cvb, g_sb, g_decay, grad_skip, grad_gain_gate, grad_step, g_cs, g_csb)
    return d_hidden + d_input, (grad_wide, grad_out), small


def body(
    hidden_in,
    cotangent,
    norm_gain,
    gate_proj,
    value_proj,
    shared_proj,
    step_proj,
    conv_value,
    conv_value_bias,
    conv_shared,
    conv_shared_bias,
    step_bias,
    decay_log,
    skip_scale,
    gate_gain,
    out_proj,
):
    wide_proj = jnp.concatenate([gate_proj, value_proj, shared_proj, step_proj], axis=2)
    stacked = (
        norm_gain,
        wide_proj,
        conv_value,
        conv_value_bias,
        conv_shared,
        conv_shared_bias,
        step_bias,
        decay_log,
        skip_scale,
        gate_gain,
        out_proj,
    )
    layer_total = norm_gain.shape[0]
    layers = [tuple(tensor[at] for tensor in stacked) for at in range(layer_total)]
    hidden = hidden_in[0]
    stored_all = []
    for weights in layers:
        hidden, stored = layer_forward(hidden, weights)
        stored_all.append(stored)
    d_hidden = cotangent[0]
    large, small = [None] * layer_total, [None] * layer_total
    for at in reversed(range(layer_total)):
        d_hidden, large[at], small[at] = layer_backward(d_hidden, stored_all[at], layers[at])
    inner = conv_value.shape[2]
    count, pairs = lax.axis_size("seq"), lax.axis_size("batch")
    shared = conv_shared.shape[2]
    cuts = (
        (0, 0, inner),
        (0, inner, 2 * inner),
        (0, 2 * inner, 2 * inner + shared),
        (1, 0, inner),
    )
    gate_sum, value_sum, shared_part, out_sum = scatter_sum(
        [grad for at in range(layer_total) for grad in large[at]], cuts, 7
    )
    out_sum = jnp.swapaxes(out_sum, 1, 2)
    groups = [[small[at][i] for at in range(layer_total)] for i in range(10)]
    totals = reduce_many(groups, ["seq", "batch"], 8)
    over_heads = [
        [group[at] for at in range(layer_total)] for group in (shared_part, totals[8], totals[9])
    ]
    shared_sum, conv_shared_sum, conv_bias_sum = reduce_many(over_heads, ["head"], 9)
    mine = gate_sum.shape[1]
    at = lax.axis_index("seq") * pairs + lax.axis_index("batch")
    step_sum = jnp.swapaxes(lax.dynamic_slice_in_dim(totals[7], at * mine, mine, axis=2), 1, 2)
    return (
        hidden[None],
        d_hidden[None],
        totals[0],
        gate_sum,
        value_sum,
        shared_sum,
        step_sum,
        totals[1],
        totals[2],
        conv_shared_sum,
        conv_bias_sum,
        totals[3],
        totals[4],
        totals[5],
        totals[6],
        out_sum,
    )


def solution(mesh):
    return jax.shard_map(
        body,
        mesh=mesh,
        in_specs=(
            P("batch", "seq", None),
            P("batch", "seq", None),
            P(),
            P(None, None, "head"),
            P(None, None, "head"),
            P(),
            P(None, None, "head"),
            P(None, None, "head"),
            P(None, "head"),
            P(),
            P(),
            P(None, "head"),
            P(None, "head"),
            P(None, "head"),
            P(None, "head"),
            P(None, "head", None),
        ),
        out_specs=(
            P("batch", "seq", None),
            P("batch", "seq", None),
            P(),
            P(None, ("seq", "batch"), "head"),
            P(None, ("seq", "batch"), "head"),
            P(None, ("seq", "batch"), None),
            P(None, ("seq", "batch"), "head"),
            P(None, None, "head"),
            P(None, "head"),
            P(),
            P(),
            P(None, "head"),
            P(None, "head"),
            P(None, "head"),
            P(None, "head"),
            P(None, "head", ("seq", "batch")),
        ),
        check_vma=False,
    )
```

time: 772 us -> 452 us (0.59)
  waiting for transfers between devices: 363 us -> 0 us
  Pallas kernels: 0 us -> 232 us
  blocking collectives: 168 us -> 0 us
  local copies, waits for them, and re-layouts: 59.5 us -> 95.1 us
  other arithmetic: 73.3 us -> 43.9 us
  starting transfers between devices: 21 us -> 0 us
  between operations: 17.9 us -> 2.14 us
  matrix products: 65.2 us -> 74.9 us
    pallas_call x0 -> x15, Pallas kernels: none -> 232 us  [the longest x1 80.5 us: scatter_sum(): pl.pallas_call(functools.partial(scatter_kernel, count, pairs, number, cu...]
    reduce_scatter x6 -> x0, waiting for transfers between devices: 131 us -> none  [the longest x2 65.4 us: reduce_grads(): lax.psum_scatter(grads[1], ('seq', 'batch'), scatter_dimension=1, tiled=T...]
    psum x3 -> x0, waiting for transfers between devices: 126 us -> none  [the longest x2 93.2 us: layer_forward(): lax.psum(jnp.dot(gated_b, out_proj, preferred_element_type=jnp.float32),...]
    unnamed x15 -> x0, waiting for transfers between devices: 96.5 us -> none
    all_gather x6 -> x0, blocking collectives: 87.8 us -> none  [prefix(): everything = jax.tree.map(lambda part: lax.all_gather(part, axis), x)]
    psum x6 -> x0, blocking collectives: 80.5 us -> none  [the longest x1 28.9 us: reduce_grads(): lax.psum((grads[0], grads[5], grads[6], grads[7], grads[8], grads[9], gra...]
    unnamed x408 -> x304, local copies, waits for them, and re-layouts: 8.93 us -> 35.2 us
    ppermute x8 -> x0, starting transfers between devices: 20.5 us -> none  [passed_along(): lax.ppermute(value, axis, [(source, source + steps) for source in range(f...]
  transfers between devices with their start and end apart: 20 -> 0, of which waited for: 13 -> 0; matrix products, arithmetic and copies ran while one was open for 12% -> 0% of each run, Pallas kernels for 0% -> 0%
where the time goes in v1:
time: 452 us; the launch traced here: 448 us
  Pallas kernels  232 us (51%)
  local copies, waits for them, and re-layouts  95.1 us (21%)
  matrix products  74.9 us (17%)
  other arithmetic  43.9 us (10%)
    pallas_call x1, Pallas kernels, scatter_sum(): pl.pallas_call(functools.partial(scatter_kernel, count, pairs, number, cu...  80.5 us
    pallas_call x4, Pallas kernels, all_reduce(): pl.pallas_call(functools.partial(all_reduce_kernel, axes, count), out_sha...  56.6 us
    pallas_call x4, Pallas kernels, chain(): pl.pallas_call(functools.partial(chain_kernel, count, step), out_shape=ja...  46.2 us
    unnamed x304, local copies, waits for them, and re-layouts  35.2 us
    pallas_call x2, Pallas kernels, reduce_many(): pl.pallas_call(functools.partial(reduce_many_kernel, axes, count, shapes,...  25.9 us
    pallas_call x4, Pallas kernels, shift(): pl.pallas_call(functools.partial(shift_kernel, lax.axis_size('seq'), step...  22.8 us
    dot_general x12, matrix products, spread(): return jnp.dot(per_head, table, precision=highest)  18.5 us
    dot_general x6, matrix products, ssd_front(): end_state = lax.dot_general(weighted, b_mat, (((0,), (0,)), ((), ())))  12.7 us

profile of v1, /device:TPU:0, one launch (start us, length us, event | category | flops | bytes accessed | tf_op | source)
XLA Modules:
  0.0 448.0 jit_solution(14220201578886031438)
XLA Ops:
  17.1 2.4 copy.196
  26.7 5.9 %shard_map.279 = f32[8,640]{1,0:T(8,128)} custom-call(f32[8,640]{1,0:T(8,128)} %slice.397.x_ref), custom_call_target="tpu_custom_call" | custom-call | tf_op jit(solution)/shard_map/pallas_call | solution.py:264
  51.4 7.2 %shard_map.280 = f32[6,64,128]{2,1,0:T(8,128)} custom-call(f32[6,1,128]{2,1,0:T(1,128)} %broadcast_in_dim.50.decay_ref, f32[6,64,128]{2,1,0:T(8,128)} %bitcast.292), custom_call_target="tpu_custom_call" | custom-call | tf_op jit(solution)/shard_map/pallas_call | solution.py:212
  58.6 2.3 multiply_reduce_fusion.25
  62.1 16.8 %shard_map.281 = f32[4,32,896]{2,1,0:T(8,128)} custom-call(f32[4,32,896]{2,1,0:T(8,128)} %bitcast.268), custom_call_target="tpu_custom_call" | custom-call | tf_op jit(solution)/shard_map/pallas_call | solution.py:84
  90.6 6.6 %shard_map.282 = f32[8,640]{1,0:T(8,128)} custom-call(f32[8,640]{1,0:T(8,128)} %slice.419.x_ref), custom_call_target="tpu_custom_call" | custom-call | tf_op jit(solution)/shard_map/pallas_call | solution.py:264
  121.8 8.9 %shard_map.283 = f32[6,64,128]{2,1,0:T(8,128)} custom-call(f32[6,1,128]{2,1,0:T(1,128)} %broadcast_in_dim.52.decay_ref, f32[6,64,128]{2,1,0:T(8,128)} %bitcast.294), custom_call_target="tpu_custom_call" | custom-call | tf_op jit(solution)/shard_map/pallas_call | solution.py:212
  130.7 2.3 multiply_reduce_fusion.24
  134.3 13.4 %shard_map.284 = f32[4,32,896]{2,1,0:T(8,128)} custom-call(f32[4,32,896]{2,1,0:T(8,128)} %bitcast.271), custom_call_target="tpu_custom_call" | custom-call | tf_op jit(solution)/shard_map/pallas_call | solution.py:84
  155.1 2.5 multiply_reduce_fusion.12
  160.6 19.5 %shard_map.285 = f32[6,64,128]{2,1,0:T(8,128)} custom-call(f32[6,1,128]{2,1,0:T(1,128)} %broadcast_in_dim.52.decay_ref, f32[6,64,128]{2,1,0:T(8,128)} %bitcast.280), custom_call_target="tpu_custom_call" | custom-call | tf_op jit(solution)/shard_map/pallas_call | solution.py:212
  186.1 2.1 fusion.66
  188.6 2.3 multiply_reduce_fusion.28
  194.2 2.5 multiply_reduce_fusion.16
  196.8 2.3 fusion.199
  211.2 5.1 %shard_map.286 = f32[8,640]{1,0:T(8,128)} custom-call(f32[8,640]{1,0:T(8,128)} %pad_maximum_fusion.8.x_ref), custom_call_target="tpu_custom_call" | custom-call | tf_op jit(solution)/shard_map/pallas_call | solution.py:264
  220.9 13.6 %shard_map.287 = f32[4,32,768]{2,1,0:T(8,128)} custom-call(f32[4,32,768]{2,1,0:T(8,128)} %fusion.2.x_ref), custom_call_target="tpu_custom_call" | custom-call | tf_op jit(solution)/shard_map/pallas_call | solution.py:84
  238.5 2.4 multiply_reduce_fusion.4
  241.1 2.1 multiply_reduce_fusion.13
  246.2 10.6 %shard_map.288 = f32[6,64,128]{2,1,0:T(8,128)} custom-call(f32[6,1,128]{2,1,0:T(1,128)} %broadcast_in_dim.50.decay_ref, f32[6,64,128]{2,1,0:T(8,128)} %bitcast.281), custom_call_target="tpu_custom_call" | custom-call | tf_op jit(solution)/shard_map/pallas_call | solution.py:212
  262.8 2.1 fusion.68
  265.3 2.2 multiply_reduce_fusion.32
  270.9 2.4 multiply_reduce_fusion.20
  277.8 2.0 fusion.15
  288.0 2.7 copy.254
  292.3 5.1 %shard_map.289 = f32[8,640]{1,0:T(8,128)} custom-call(f32[8,640]{1,0:T(8,128)} %pad_maximum_fusion.7.x_ref), custom_call_target="tpu_custom_call" | custom-call | tf_op jit(solution)/shard_map/pallas_call | solution.py:264
  301.0 12.7 %shard_map.290 = f32[4,32,768]{2,1,0:T(8,128)} custom-call(f32[4,32,768]{2,1,0:T(8,128)} %fusion.x_ref), custom_call_target="tpu_custom_call" | custom-call | tf_op jit(solution)/shard_map/pallas_call | solution.py:84
  318.9 13.9 %shard_map.291 = (f32[2,768]{1,0:T(2,128)}, f32[2,4,384]{2,1,0:T(4,128)}, f32[2,384]{1,0:T(2,128)}, f32[2,6]{1,0:T(2,128)}, f32[2,6]{1,0:T(2,128)}, /*index=5*/f...) custom-call(f32[1,768]{1,0:T(1,128)} %reshape.497.refs_0_, ...), custom_call_target="tpu_custom_call" | custom-call | tf_op jit(solution)/shard_map/pallas_call | solution.py:147
  338.3 2.2 fusion.59.refs_0_
  340.5 2.3 fusion.62
  342.8 80.5 %shard_map.292 = (f32[2,96,384]{2,1,0:T(8,128)}, f32[2,96,384]{2,1,0:T(8,128)}, f32[2,96,256]{2,1,0:T(8,128)}, f32[2,96,384]{2,1,0:T(8,128)}) custom-call(f32[4,2,96,1024]{3,2,1,0:T(8,128)} %fusion.59.refs_0_, f32[4,2,96,384]{3,2,1,0:T(8,128)} %bitcast.265, f32[4,2,96,1024]{3,2,1,0:T(8,128)} %bitcast.263, f32[4,2,96,384]{3,2,1,0:T(8,128)} %bitcast.264), custom_call_target="tpu_custom_call" | custom-call | tf_op jit(solution)/shard_map/pallas_call | solution.py:422
  425.0 12.0 %shard_map.293 = (f32[2,96,256]{2,1,0:T(8,128)}, f32[2,4,256]{2,1,0:T(4,128)}, f32[2,256]{1,0:T(2,128)}) custom-call(f32[96,256]{1,0:T(8,128)} %get-tuple-element.206.refs_0_, f32[96,256]{1,0:T(8,128)} %get-tuple-element.205.refs_1_, f32[4,256]{1,0:T(4,128)} %get-tuple-element.224.refs_2_, f32[4,256]{1,0:T(4,128)} %get-tuple-element.223.refs_3_, ...), custom_call_target="tpu_custom_call" | custom-call | tf_op jit(solution)/shard_map/pallas_call | solution.py:147
  (464 shorter events, 174.7 us)
Async XLA Ops:
  4.9 20.4 %copy-start.134 = (f32[6]{0:T(128)}, f32[6]{0:T(128)S(1)}, u32[]{:S(2)}) copy-start(f32[6]{0:T(128)S(1)} %get-tuple-element.253) | copy-start | bytes 76
  4.9 30.8 %copy-start.92 = (f32[6]{0:T(128)}, f32[6]{0:T(128)S(1)}, u32[]{:S(2)}) copy-start(f32[6]{0:T(128)S(1)} %get-tuple-element.242) | copy-start | bytes 76
  13.4 29.0 %copy-start.65 = (f32[384]{0:T(512)}, f32[384]{0:T(512)S(1)}, u32[]{:S(2)}) copy-start(f32[384]{0:T(512)S(1)} %get-tuple-element.154) | copy-start | bytes 4612
  13.4 29.0 %copy-start.67 = (f32[384]{0:T(512)}, f32[384]{0:T(512)S(1)}, u32[]{:S(2)}) copy-start(f32[384]{0:T(512)S(1)} %get-tuple-element.155) | copy-start | bytes 4612
  13.4 29.0 %copy-start.69 = (f32[384]{0:T(512)}, f32[384]{0:T(512)S(1)}, u32[]{:S(2)}) copy-start(f32[384]{0:T(512)S(1)} %get-tuple-element.156) | copy-start | bytes 4612
  13.4 29.0 %copy-start.71 = (f32[384]{0:T(512)}, f32[384]{0:T(512)S(1)}, u32[]{:S(2)}) copy-start(f32[384]{0:T(512)S(1)} %get-tuple-element.157) | copy-start | bytes 4612
  13.4 99.4 %copy-start.73 = (f32[384]{0:T(512)}, f32[384]{0:T(512)S(1)}, u32[]{:S(2)}) copy-start(f32[384]{0:T(512)S(1)} %get-tuple-element.152) | copy-start | bytes 4612
  88.3 21.2 %copy-start.91 = (f32[1,1,256]{2,1,0:T(1,128)S(1)}, f32[1,1,256]{2,1,0:T(1,128)}, u32[]{:S(2)}) copy-start(f32[1,1,256]{2,1,0:T(1,128)} %get-tuple-element.225) | copy-start | bytes 3076
  89.1 23.7 %copy-start.74 = (f32[384]{0:T(512)S(1)}, f32[384]{0:T(512)}, u32[]{:S(2)}) copy-start(f32[384]{0:T(512)} %get-tuple-element.153) | copy-start | bytes 4612
  89.1 23.7 %copy-start.75 = (f32[384]{0:T(512)S(1)}, f32[384]{0:T(512)}, u32[]{:S(2)}) copy-start(f32[384]{0:T(512)} %get-tuple-element.158) | copy-start | bytes 4612
  89.1 23.6 %copy-start.76 = (f32[384]{0:T(512)S(1)}, f32[384]{0:T(512)}, u32[]{:S(2)}) copy-start(f32[384]{0:T(512)} %get-tuple-element.159) | copy-start | bytes 4612
  114.5 16.2 %copy-start.137 = (f32[384]{0:T(512)S(1)}, f32[384]{0:T(512)}, u32[]{:S(2)}) copy-start(f32[384]{0:T(512)} %convolution_reduce_fusion) | copy-start | bytes 4612
  158.9 27.2 %copy-start.82 = (pred[128,128]{1,0:T(8,128)(4,1)S(1)}, pred[128,128]{1,0:T(8,128)(4,1)}, u32[]{:S(2)}) copy-start(pred[128,128]{1,0:T(8,128)(4,1)} %iota_compare_fusion) | copy-start | bytes 49156
  158.9 27.2 %copy-start.110 = (f32[128,6]{0,1:T(8,128)S(1)}, f32[128,6]{0,1:T(8,128)}, u32[]{:S(2)}) copy-start(f32[128,6]{0,1:T(8,128)} %fusion.157) | copy-start | bytes 9220
  219.7 16.7 %copy-start.103 = (f32[128]{0:T(128)S(1)}, f32[128]{0:T(128)}, u32[]{:S(2)}) copy-start(f32[128]{0:T(128)} %copy-done.102) | copy-start | bytes 1540
  220.9 17.6 %copy-start.133 = (f32[128]{0:T(128)S(1)}, f32[128]{0:T(128)}, u32[]{:S(2)}) copy-start(f32[128]{0:T(128)} %copy-done.132) | copy-start | bytes 1540
  220.9 17.6 %copy-start.100 = (f32[128]{0:T(128)S(1)}, f32[128]{0:T(128)}, u32[]{:S(2)}) copy-start(f32[128]{0:T(128)} %copy-done.99) | copy-start | bytes 1540
  244.4 18.3 %copy-start.83 = (pred[128,128]{1,0:T(8,128)(4,1)S(1)}, pred[128,128]{1,0:T(8,128)(4,1)}, u32[]{:S(2)}) copy-start(pred[128,128]{1,0:T(8,128)(4,1)} %iota_compare_fusion) | copy-start | bytes 49156
  244.4 18.3 %copy-start.107 = (f32[128,6]{0,1:T(8,128)S(1)}, f32[128,6]{0,1:T(8,128)}, u32[]{:S(2)}) copy-start(f32[128,6]{0,1:T(8,128)} %copy-done.106) | copy-start | bytes 9220
  244.4 18.3 %copy-start.108 = (f32[6,128]{1,0:T(8,128)S(1)}, f32[6,128]{1,0:T(8,128)}, u32[]{:S(2)}) copy-start(f32[6,128]{1,0:T(8,128)} %copy.205) | copy-start | bytes 9220
  316.9 19.9 %copy-start.43 = (f32[128,384]{1,0:T(8,128)S(1)}, f32[128,384]{1,0:T(8,128)}, u32[]{:S(2)}) copy-start(f32[128,384]{1,0:T(8,128)} %copy-done.41) | copy-start | bytes 589828
  316.9 19.9 %copy-start.79 = (f32[384]{0:T(512)S(1)}, f32[384]{0:T(512)}, u32[]{:S(2)}) copy-start(f32[384]{0:T(512)} %get-tuple-element.163) | copy-start | bytes 4612
  317.0 19.9 %copy-start.120 = (f32[128]{0:T(128)S(1)}, f32[128]{0:T(128)}, u32[]{:S(2)}) copy-start(f32[128]{0:T(128)} %copy-done.118) | copy-start | bytes 1540
  317.2 21.1 %copy-start.23 = (bf16[128,640]{1,0:T(8,128)(2,1)S(1)}, bf16[128,640]{1,0:T(8,128)(2,1)}, u32[]{:S(2)}) copy-start(bf16[128,640]{1,0:T(8,128)(2,1)} %copy-done.22) | copy-start | bytes 491524
  342.7 94.3 %copy-start.98 = (f32[2,768]{1,0:T(2,128)S(1)}, f32[2,768]{1,0:T(2,128)}, u32[]{:S(2)}) copy-start(f32[2,768]{1,0:T(2,128)} %get-tuple-element.279) | copy-start | bytes 18436
  423.3 19.4 %copy-start.84 = (f32[2,4,384]{2,1,0:T(4,128)S(1)}, f32[2,4,384]{2,1,0:T(4,128)}, u32[]{:S(2)}) copy-start(f32[2,4,384]{2,1,0:T(4,128)} %get-tuple-element.284) | copy-start | bytes 36868
  423.3 20.0 %copy-start.117 = (f32[2,384]{1,0:T(2,128)S(1)}, f32[2,384]{1,0:T(2,128)}, u32[]{:S(2)}) copy-start(f32[2,384]{1,0:T(2,128)} %get-tuple-element.285) | copy-start | bytes 9220
  423.3 21.8 %copy-start.127 = (f32[2,6]{1,0:T(2,128)S(1)}, f32[2,6]{1,0:T(2,128)}, u32[]{:S(2)}) copy-start(f32[2,6]{1,0:T(2,128)} %get-tuple-element.288) | copy-start | bytes 148
  423.3 22.3 %copy-start.126 = (f32[2,6]{1,0:T(2,128)S(1)}, f32[2,6]{1,0:T(2,128)}, u32[]{:S(2)}) copy-start(f32[2,6]{1,0:T(2,128)} %get-tuple-element.289) | copy-start | bytes 148
  423.3 22.9 %copy-start.125 = (f32[2,6]{1,0:T(2,128)S(1)}, f32[2,6]{1,0:T(2,128)}, u32[]{:S(2)}) copy-start(f32[2,6]{1,0:T(2,128)} %get-tuple-element.290) | copy-start | bytes 148
  423.3 23.4 %copy-start.116 = (f32[2,384]{1,0:T(2,128)S(1)}, f32[2,384]{1,0:T(2,128)}, u32[]{:S(2)}) copy-start(f32[2,384]{1,0:T(2,128)} %get-tuple-element.291) | copy-start | bytes 9220
  423.3 24.0 %copy-start.51 = (f32[2,96,384]{2,1,0:T(8,128)S(1)}, f32[2,96,384]{2,1,0:T(8,128)}, u32[]{:S(2)}) copy-start(f32[2,96,384]{2,1,0:T(8,128)} %get-tuple-element.57) | copy-start | bytes 884740
  (107 other events, 533.3 us)
